TPU v7x, 32 devices: a whole 2x2x4 slice. The times are simulated.
32 devices in a mesh: energy: 8 (over y, x, core), elem: 4 (over z).
Axes of the slice: x: 2, y: 2, z: 4, core: 2. Of those that a mesh axis runs over, the one named last changes fastest.
Arguments:
- g_lesser: bfloat16 [2, 512, 2048], P(None, 'energy', 'elem'), may hold values from -6 to 6
- g_greater: bfloat16 [2, 512, 2048], P(None, 'energy', 'elem'), may hold values from -6 to 6
- send_rows: int32 [4, 8, 4, 32], P('elem'), may hold values from 0 to 63, as said below
- partner_slot: int32 [2048], P('elem'), may hold values from 0 to 127, as said below
Outputs:
- polarization_lesser: bfloat16 [2, 512, 2048], P(None, 'energy', 'elem')
- polarization_greater: bfloat16 [2, 512, 2048], P(None, 'energy', 'elem')
Inputs may be any that keep to these rules, and one draw needn't show every extreme that they name: partner is an involution on the elements that keeps the element piece n. The groups fall into two halves of 2 groups; for a sending group b and element piece n, send_rows[b, n, a, :] lists 32 distinct rows when a lies in b's half (b itself included) and zeros otherwise; every row of that piece of the sender appears exactly once over all receivers of its half. `partner_slot`: every slot named points into a receiving group's half and to a slot that carries a row; the 64 elements of one element piece of a group name 64 distinct slots.
All inputs are finite; a program needn't handle non-finite values.
Results may differ from a plain program's by a relative error of at most 0.001.
Values may be sent and summed in bfloat16 or wider, within the bound.
No kernel may reach another device: no remote copies, remote signals or barrier semaphores. Data moves between devices by JAX's collectives and lax.ppermute only.
A program may use at most 64 MiB of HBM per device.

v0:
```python
from functools import partial
import math
import jax
import jax.numpy as jnp
from jax import lax
from jax.sharding import PartitionSpec as P


def factor_pair(length):
    divisor = math.isqrt(length)
    while length % divisor:
        divisor -= 1
    return divisor


def phase_tables(rows_count, cols_count, modulus, inverse):
    sign_factor = 1.0 if inverse else -1.0
    left_index = jnp.arange(rows_count, dtype=jnp.int32)
    right_index = jnp.arange(cols_count, dtype=jnp.int32)
    phases = (left_index[:, None] * right_index[None, :] % modulus).astype(jnp.float32) * (
        2.0 * math.pi / modulus
    )
    return (jnp.cos(phases), sign_factor * jnp.sin(phases))


def transform(real_part, imag_part, inverse):
    signals, length, width = real_part.shape
    first_size = factor_pair(length)
    second_size = length // first_size
    cos_first, sin_first = phase_tables(first_size, first_size, first_size, inverse)
    cos_twist, sin_twist = phase_tables(first_size, second_size, length, inverse)
    cos_second, sin_second = phase_tables(second_size, second_size, second_size, inverse)
    product = partial(jnp.einsum, precision=lax.Precision.HIGHEST)
    real_grid = real_part.reshape(signals, first_size, second_size, width)
    imag_grid = imag_part.reshape(signals, first_size, second_size, width)
    inner_re = product("ka,sabe->skbe", cos_first, real_grid) - product(
        "ka,sabe->skbe", sin_first, imag_grid
    )
    inner_im = product("ka,sabe->skbe", cos_first, imag_grid) + product(
        "ka,sabe->skbe", sin_first, real_grid
    )
    twist_cos = cos_twist[None, :, :, None]
    twist_sin = sin_twist[None, :, :, None]
    twist_re = inner_re * twist_cos - inner_im * twist_sin
    twist_im = inner_re * twist_sin + inner_im * twist_cos
    outer_re = product("qb,skbe->sqke", cos_second, twist_re) - product(
        "qb,skbe->sqke", sin_second, twist_im
    )
    outer_im = product("qb,skbe->sqke", cos_second, twist_im) + product(
        "qb,skbe->sqke", sin_second, twist_re
    )
    return (outer_re.reshape(signals, length, width), outer_im.reshape(signals, length, width))


def reverse_energy(values):
    return jnp.roll(jnp.flip(values, axis=1), 1, axis=1)


def shards(g_lesser, g_greater, send_rows, partner_slot):
    piece_index = lax.axis_index("energy")
    energy_count = lax.axis_size("energy")
    group_rows = partner_slot.shape[0]
    elem_dev = group_rows // energy_count
    own_lesser, own_greater = (
        lax.all_to_all(g_lesser, "energy", split_axis=2, concat_axis=1, tiled=True),
        lax.all_to_all(g_greater, "energy", split_axis=2, concat_axis=1, tiled=True),
    )
    own_rows = jnp.stack([own_lesser, own_greater])
    partner_columns = lax.dynamic_slice_in_dim(partner_slot, piece_index * elem_dev, elem_dev, 0)
    chosen_rows = lax.dynamic_index_in_dim(send_rows[0], piece_index, 0, keepdims=False).reshape(-1)
    outgoing = jnp.take(own_rows, chosen_rows, axis=3)
    incoming = lax.all_to_all(outgoing, "elem", split_axis=3, concat_axis=3, tiled=True)
    partner_rows = jnp.take(incoming, partner_columns, axis=3)
    signals = jnp.concatenate([own_rows, partner_rows], 0).astype(jnp.float32)
    spec_re, spec_im = transform(signals[:, 0], signals[:, 1], False)
    near_re = spec_re[:2]
    near_im = spec_im[:2]
    far_re = reverse_energy(jnp.stack([spec_re[3], spec_re[2]]))
    far_im = reverse_energy(jnp.stack([spec_im[3], spec_im[2]]))
    prod_re = near_re * far_re - near_im * far_im
    prod_im = near_re * far_im + near_im * far_re
    back_re, back_im = transform(prod_re, prod_im, True)
    length = back_re.shape[1]
    factor = 1.0 / (length * math.sqrt(length))
    result = jnp.stack([factor * back_im, -factor * back_re], 1).astype(jnp.bfloat16)
    lesser_out, greater_out = (
        lax.all_to_all(result[0], "energy", split_axis=1, concat_axis=2, tiled=True),
        lax.all_to_all(result[1], "energy", split_axis=1, concat_axis=2, tiled=True),
    )
    return (lesser_out, greater_out)


def solution(mesh):
    in_specs = (
        P(None, "energy", "elem"),
        P(None, "energy", "elem"),
        P("elem", None, None, None),
        P("elem"),
    )
    out_specs = (P(None, "energy", "elem"), P(None, "energy", "elem"))
    return jax.shard_map(shards, mesh=mesh, in_specs=in_specs, out_specs=out_specs, check_vma=False)
```

profile of v0, /device:TPU:0, one launch (start us, length us, event | category | flops | bytes accessed | tf_op | source)
XLA Modules:
  0.0 93.1 jit_solution(4972418240594326676)
XLA Ops:
  0.6 1.1 %copy.86 = bf16[2,64,512]{1,0,2:T(2,128)(2,1)S(1)} copy(bf16[2,64,512]{2,1,0:T(8,128)(2,1)} %param.4) | data formatting | bytes 262144 | tf_op args[0]
  1.7 0.9 reshape.175
  2.6 5.3 %all-to-all-start = ((bf16[8,2,4096]{2,1,0:T(2,128)(2,1)}), bf16[8,2,4096]{2,1,0:T(2,128)(2,1)S(1)}, u32[]{:S(2)}, u32[]{:S(2)}) async-start(bf16[8,2,4096]{2,1,0:T(2,128)(2,1)} %reshape.175), calls=%async_computation | async-start | bytes 262144 | tf_op jit(solution)/shard_map/all_to_all | solution.py:65
  8.3 0.9 reshape.173
  9.2 4.3 %all-to-all-done = bf16[8,2,4096]{2,1,0:T(2,128)(2,1)S(1)} async-done(((bf16[8,2,4096]{2,1,0:T(2,128)(2,1)}), bf16[8,2,4096]{2,1,0:T(2,128)(2,1)S(1)}, u32[]{:S(2)}, u32[]{:S(2)}) %all-to-all-start) | async-done | bytes 131104 | tf_op jit(solution)/shard_map/all_to_all | solution.py:65
  13.5 3.4 %all-to-all-start.1 = ((bf16[8,2,4096]{2,1,0:T(2,128)(2,1)}), bf16[8,2,4096]{2,1,0:T(2,128)(2,1)S(1)}, u32[]{:S(2)}, u32[]{:S(2)}) async-start(bf16[8,2,4096]{2,1,0:T(2,128)(2,1)} %reshape.173), calls=%async_computation.1 | async-start | bytes 262144 | tf_op jit(solution)/shard_map/all_to_all | solution.py:66
  17.6 4.7 %all-to-all-done.1 = bf16[8,2,4096]{2,1,0:T(2,128)(2,1)S(1)} async-done(((bf16[8,2,4096]{2,1,0:T(2,128)(2,1)}), bf16[8,2,4096]{2,1,0:T(2,128)(2,1)S(1)}, u32[]{:S(2)}, u32[]{:S(2)}) %all-to-all-start.1) | async-done | bytes 131104 | tf_op jit(solution)/shard_map/all_to_all | solution.py:66
  23.1 0.4 pad_maximum_fusion.4
  23.4 1.7 %gather_fusion = bf16[128,2,2,512]{3,2,1,0:T(2,128)(2,1)S(1)} fusion(bf16[2,2,512,64]{2,1,3,0:T(2,128)(2,1)S(1)} %pad_maximum_fusion.4, s32[1024]{0:T(1024)S(1)} %pad_clamp_fusion.1), kind=kCustom, calls=%fused_computation | custom fusion | bytes 1049088 | tf_op jit(solution)/shard_map/jit(_take)/gather | solution.py:71
  25.1 1.4 %fusion.22 = bf16[2,2,512,128]{2,1,0,3:T(2,128)(2,1)} fusion(bf16[128,2,2,512]{3,2,1,0:T(2,128)(2,1)S(1)} %gather_fusion, pred[128]{0:T(512)(128)(4,1)S(1)} %compare_and_fusion), kind=kLoop, calls=%fused_computation.49 | loop fusion | flops 262144 | bytes 1048704 | tf_op jit(solution)/shard_map/jit(_take)/select_n | solution.py:71
  26.5 4.9 %all-to-all-start.2 = ((bf16[2,2,512,128]{2,1,0,3:T(2,128)(2,1)}), bf16[2,2,512,128]{2,1,0,3:T(2,128)(2,1)S(1)}, u32[]{:S(2)}, u32[]{:S(2)}) async-start(bf16[2,2,512,128]{2,1,0,3:T(2,128)(2,1)} %fusion.22), calls=%async_computation.2 | async-start | bytes 1048576 | tf_op jit(solution)/shard_map/all_to_all | solution.py:72
  31.4 0.8 compare_and_fusion.1
  32.6 13.1 %all-to-all-done.2 = bf16[2,2,512,128]{2,1,0,3:T(2,128)(2,1)S(1)} async-done(((bf16[2,2,512,128]{2,1,0,3:T(2,128)(2,1)}), bf16[2,2,512,128]{2,1,0,3:T(2,128)(2,1)S(1)}, u32[]{:S(2)}, u32[]{:S(2)}) %all-to-all-start.2) | async-done | bytes 524320 | tf_op jit(solution)/shard_map/all_to_all | solution.py:72
  46.0 1.1 %gather_fusion.1 = bf16[64,2,2,512]{3,2,1,0:T(2,128)(2,1)S(1)} fusion(bf16[2,2,512,128]{2,1,3,0:T(2,128)(2,1)S(1)} %copy.92, s32[1024]{0:T(1024)S(1)} %pad_clamp_fusion), kind=kCustom, calls=%fused_computation.1 | custom fusion | bytes 524544 | tf_op jit(solution)/shard_map/jit(_take)/gather | solution.py:73
  47.5 0.7 pad_maximum_fusion.2
  48.2 0.7 fusion.180
  48.9 0.5 copy.95
  49.5 0.7 copy.97
  50.2 0.6 fusion.35
  50.8 0.6 fusion.39
  51.4 0.6 fusion.3
  52.1 0.9 multiply_add_fusion
  53.0 1.4 %fusion.12 = f32[4,16,64,32]{2,3,1,0:T(8,128)S(1)} fusion(f32[4,16,32,64]{3,1,2,0:T(8,128)S(1)} %get-tuple-element.4), kind=kOutput, calls=%fused_computation.25 | convolution fusion | flops 50345984 | bytes 1048576 | tf_op jit(solution)/shard_map/qb,skbe->sqke/dot_general | solution.py:49
  54.4 1.4 %fusion.16 = f32[4,16,64,32]{2,3,1,0:T(8,128)S(1)} fusion(f32[4,16,32,64]{3,1,2,0:T(8,128)S(1)} %get-tuple-element.5), kind=kOutput, calls=%fused_computation.29 | convolution fusion | flops 50345984 | bytes 1048576 | tf_op jit(solution)/shard_map/qb,skbe->sqke/dot_general | solution.py:46
  55.8 1.4 %fusion.1 = f32[4,32,16,64]{3,1,2,0:T(8,128)S(1)} fusion(f32[4,16,64,32]{2,3,1,0:T(8,128)S(1)} %fusion.16, f32[4,16,32,64]{3,1,2,0:T(8,128)S(1)} %get-tuple-element.4), kind=kOutput, calls=%fused_computation.5 | convolution fusion | flops 50478080 | bytes 1572864 | tf_op jit(solution)/shard_map/qb,skbe->sqke/dot_general | solution.py:46
  57.2 1.0 %copy-done.1 = f32[4,32,16,64]{3,1,2,0:T(8,128)} copy-done((f32[4,32,16,64]{3,1,2,0:T(8,128)}, f32[4,32,16,64]{3,1,2,0:T(8,128)S(1)}, u32[]{:S(2)}) %copy-start.1) | copy-done | bytes 524312
  58.2 1.4 %fusion = f32[4,32,16,64]{3,1,2,0:T(8,128)S(1)} fusion(f32[4,16,64,32]{2,3,1,0:T(8,128)S(1)} %fusion.12, f32[4,16,32,64]{3,1,2,0:T(8,128)S(1)} %get-tuple-element.5), kind=kOutput, calls=%fused_computation.3 | convolution fusion | flops 50478080 | bytes 1572864 | tf_op jit(solution)/shard_map/qb,skbe->sqke/dot_general | solution.py:49
  59.6 1.0 %copy-done.2 = f32[4,32,16,64]{3,1,2,0:T(8,128)} copy-done((f32[4,32,16,64]{3,1,2,0:T(8,128)}, f32[4,32,16,64]{3,1,2,0:T(8,128)S(1)}, u32[]{:S(2)}) %copy-start.2) | copy-done | bytes 524312
  60.8 0.9 slice-done
  62.2 0.7 slice.80
  63.1 0.9 slice-done.1
  64.5 0.9 slice.89
  65.7 0.9 fusion.33
  66.6 0.9 fusion.29
  67.5 0.9 fusion.7
  68.4 1.1 %multiply_subtract_fusion.1 = (f32[2,16,32,64]{3,1,2,0:T(8,128)S(1)}, f32[2,16,32,64]{3,1,2,0:T(8,128)S(1)}) fusion(f32[2,16,32,64]{3,1,2,0:T(8,128)S(1)} %fusion.7, f32[16,32]{0,1:T(8,128)S(1)} %get-tuple-element.19, f32[16,32]{0,1:T(8,128)S(1)} %fusion.90, f32[2,32,64,16]{2,3,1,0:T(8,128)S(1)} %fusion.29, f32[2,16,32,64]{3,2,1,0:T(8,128)S(1)} %get-tuple-element.6), kind=kOutput, calls=%fused_computation.47 | convolution fusion | flops 13045248 | bytes 1314816 | tf_op jit(solution)/shard_map/ka,sabe->skbe/dot_general | solution.py:39
  69.5 0.8 fusion.23
  70.3 0.8 fusion.27
  71.0 0.8 fusion.10
  71.8 0.8 fusion.11
  73.2 0.9 reshape.179
  74.1 3.4 %all-to-all-start.4 = ((bf16[8,2,4096]{2,1,0:T(2,128)(2,1)}), bf16[8,2,4096]{2,1,0:T(2,128)(2,1)S(1)}, u32[]{:S(2)}, u32[]{:S(2)}) async-start(bf16[8,2,4096]{2,1,0:T(2,128)(2,1)} %reshape.179), calls=%async_computation.4 | async-start | bytes 262144 | tf_op jit(solution)/shard_map/all_to_all | solution.py:88
  77.8 0.9 reshape.177
  78.7 4.3 %all-to-all-done.4 = bf16[8,2,4096]{2,1,0:T(2,128)(2,1)S(1)} async-done(((bf16[8,2,4096]{2,1,0:T(2,128)(2,1)}), bf16[8,2,4096]{2,1,0:T(2,128)(2,1)S(1)}, u32[]{:S(2)}, u32[]{:S(2)}) %all-to-all-start.4) | async-done | bytes 131104 | tf_op jit(solution)/shard_map/all_to_all | solution.py:88
  83.0 3.4 %all-to-all-start.3 = ((bf16[8,2,4096]{2,1,0:T(2,128)(2,1)}), bf16[8,2,4096]{2,1,0:T(2,128)(2,1)S(1)}, u32[]{:S(2)}, u32[]{:S(2)}) async-start(bf16[8,2,4096]{2,1,0:T(2,128)(2,1)} %reshape.177), calls=%async_computation.3 | async-start | bytes 262144 | tf_op jit(solution)/shard_map/all_to_all | solution.py:87
  86.8 0.9 all_to_all.65
  87.6 4.2 %all-to-all-done.3 = bf16[8,2,4096]{2,1,0:T(2,128)(2,1)S(1)} async-done(((bf16[8,2,4096]{2,1,0:T(2,128)(2,1)}), bf16[8,2,4096]{2,1,0:T(2,128)(2,1)S(1)}, u32[]{:S(2)}, u32[]{:S(2)}) %all-to-all-start.3) | async-done | bytes 131104 | tf_op jit(solution)/shard_map/all_to_all | solution.py:87
  92.2 0.9 all_to_all.61
  (52 shorter events, 6.4 us)
Async XLA Ops:
  0.6 7.3 %copy-start = (s32[1,8,4,32]{3,2,1,0:T(4,128)S(1)}, s32[1,8,4,32]{3,2,1,0:T(4,128)}, u32[]{:S(2)}) copy-start(s32[1,8,4,32]{3,2,1,0:T(4,128)} %param.6) | copy-start | bytes 12292
  2.6 5.5 %copy-start.3 = (bf16[2,64,512]{2,1,0:T(8,128)(2,1)S(1)}, bf16[2,64,512]{2,1,0:T(8,128)(2,1)}, u32[]{:S(2)}) copy-start(bf16[2,64,512]{2,1,0:T(8,128)(2,1)} %param.5) | copy-start | bytes 393220
  2.6 10.8 %all-to-all-start = ((bf16[8,2,4096]{2,1,0:T(2,128)(2,1)}), bf16[8,2,4096]{2,1,0:T(2,128)(2,1)S(1)}, u32[]{:S(2)}, u32[]{:S(2)}) async-start(bf16[8,2,4096]{2,1,0:T(2,128)(2,1)} %reshape.175), calls=%async_computation | async-start | bytes 262144 | tf_op jit(solution)/shard_map/all_to_all | solution.py:65
  13.5 8.8 %all-to-all-start.1 = ((bf16[8,2,4096]{2,1,0:T(2,128)(2,1)}), bf16[8,2,4096]{2,1,0:T(2,128)(2,1)S(1)}, u32[]{:S(2)}, u32[]{:S(2)}) async-start(bf16[8,2,4096]{2,1,0:T(2,128)(2,1)} %reshape.173), calls=%async_computation.1 | async-start | bytes 262144 | tf_op jit(solution)/shard_map/all_to_all | solution.py:66
  26.5 19.2 %all-to-all-start.2 = ((bf16[2,2,512,128]{2,1,0,3:T(2,128)(2,1)}), bf16[2,2,512,128]{2,1,0,3:T(2,128)(2,1)S(1)}, u32[]{:S(2)}, u32[]{:S(2)}) async-start(bf16[2,2,512,128]{2,1,0,3:T(2,128)(2,1)} %fusion.22), calls=%async_computation.2 | async-start | bytes 1048576 | tf_op jit(solution)/shard_map/all_to_all | solution.py:72
  57.2 1.0 %copy-start.1 = (f32[4,32,16,64]{3,1,2,0:T(8,128)}, f32[4,32,16,64]{3,1,2,0:T(8,128)S(1)}, u32[]{:S(2)}) copy-start(f32[4,32,16,64]{3,1,2,0:T(8,128)S(1)} %fusion.1) | copy-start | bytes 1572868
  59.6 1.0 %copy-start.2 = (f32[4,32,16,64]{3,1,2,0:T(8,128)}, f32[4,32,16,64]{3,1,2,0:T(8,128)S(1)}, u32[]{:S(2)}) copy-start(f32[4,32,16,64]{3,1,2,0:T(8,128)S(1)} %fusion) | copy-start | bytes 1572868
  60.6 1.0 %slice-start = ((f32[4,32,16,64]{3,1,2,0:T(8,128)}), f32[2,32,16,64]{3,1,2,0:T(8,128)S(1)}, s32[]{:S(2)}) async-start(f32[4,32,16,64]{3,1,2,0:T(8,128)} %copy-done.1), calls=%async_computation.5 | async-start | bytes 1048576 | tf_op jit(solution)/shard_map/slice | solution.py:76
  62.9 1.0 %slice-start.1 = ((f32[4,32,16,64]{3,1,2,0:T(8,128)}), f32[2,32,16,64]{3,1,2,0:T(8,128)S(1)}, s32[]{:S(2)}) async-start(f32[4,32,16,64]{3,1,2,0:T(8,128)} %copy-done.2), calls=%async_computation.6 | async-start | bytes 1048576 | tf_op jit(solution)/shard_map/slice | solution.py:77
  74.1 8.8 %all-to-all-start.4 = ((bf16[8,2,4096]{2,1,0:T(2,128)(2,1)}), bf16[8,2,4096]{2,1,0:T(2,128)(2,1)S(1)}, u32[]{:S(2)}, u32[]{:S(2)}) async-start(bf16[8,2,4096]{2,1,0:T(2,128)(2,1)} %reshape.179), calls=%async_computation.4 | async-start | bytes 262144 | tf_op jit(solution)/shard_map/all_to_all | solution.py:88
  83.0 8.8 %all-to-all-start.3 = ((bf16[8,2,4096]{2,1,0:T(2,128)(2,1)}), bf16[8,2,4096]{2,1,0:T(2,128)(2,1)S(1)}, u32[]{:S(2)}, u32[]{:S(2)}) async-start(bf16[8,2,4096]{2,1,0:T(2,128)(2,1)} %reshape.177), calls=%async_computation.3 | async-start | bytes 262144 | tf_op jit(solution)/shard_map/all_to_all | solution.py:87
where the time goes:
time: 93.8 us; the launch traced here: 93.1 us
  waiting for transfers between devices  30.5 us (33%)
  local copies, waits for them, and re-layouts  21.7 us (23%)
  starting transfers between devices  20.3 us (22%)
  matrix products  15.2 us (16%)
  other arithmetic  4.33 us (5%)
  between operations  1.15 us (1%)
    all_to_all x1, waiting for transfers between devices, shards(): lax.all_to_all(outgoing, 'elem', split_axis=3, concat_axis=3, tiled=True)  13.1 us
    unnamed x18, local copies, waits for them, and re-layouts  7.64 us
    all_to_all x1, starting transfers between devices, shards(): lax.all_to_all(g_lesser, 'energy', split_axis=2, concat_axis=1, tiled=True)  5.3 us
    all_to_all x1, starting transfers between devices, shards(): lax.all_to_all(outgoing, 'elem', split_axis=3, concat_axis=3, tiled=True)  4.87 us
    all_to_all x1, waiting for transfers between devices, shards(): lax.all_to_all(g_greater, 'energy', split_axis=2, concat_axis=1, tiled=True)  4.68 us
    all_to_all x1, waiting for transfers between devices, shards(): lax.all_to_all(result[1], 'energy', split_axis=1, concat_axis=2, tiled=True)  4.29 us
    all_to_all x1, waiting for transfers between devices, shards(): lax.all_to_all(g_lesser, 'energy', split_axis=2, concat_axis=1, tiled=True)  4.26 us
    all_to_all x1, waiting for transfers between devices, shards(): lax.all_to_all(result[0], 'energy', split_axis=1, concat_axis=2, tiled=True)  4.19 us
  transfers between devices with their start and end apart: 5, of which 5 were waited for; matrix products, arithmetic and copies ran while one was open for 5% of the time, Pallas kernels for 0%

commit v1 on v0

--- a/solution.py
+++ b/solution.py
@@ -4,6 +4,22 @@
 import jax.numpy as jnp
 from jax import lax
 from jax.sharding import PartitionSpec as P
+
+
+def swapped_with_each(x, axis, split, join):
+    ways, here = (lax.axis_size(axis), lax.axis_index(axis))
+    width = x.shape[split] // ways
+    shape = list(x.shape)
+    shape[split] = width
+    height = shape[join]
+    shape[join] = height * ways
+    full = jnp.zeros(shape, x.dtype)
+    for mask in range(ways):
+        part = lax.dynamic_slice_in_dim(x, (here ^ mask) * width, width, axis=split)
+        if mask:
+            part = lax.ppermute(part, axis, [(d, d ^ mask) for d in range(ways)])
+        full = lax.dynamic_update_slice_in_dim(full, part, (here ^ mask) * height, axis=join)
+    return full
 
 
 def factor_pair(length):
@@ -69,7 +85,7 @@
     partner_columns = lax.dynamic_slice_in_dim(partner_slot, piece_index * elem_dev, elem_dev, 0)
     chosen_rows = lax.dynamic_index_in_dim(send_rows[0], piece_index, 0, keepdims=False).reshape(-1)
     outgoing = jnp.take(own_rows, chosen_rows, axis=3)
-    incoming = lax.all_to_all(outgoing, "elem", split_axis=3, concat_axis=3, tiled=True)
+    incoming = swapped_with_each(outgoing, "elem", 3, 3)
     partner_rows = jnp.take(incoming, partner_columns, axis=3)
     signals = jnp.concatenate([own_rows, partner_rows], 0).astype(jnp.float32)
     spec_re, spec_im = transform(signals[:, 0], signals[:, 1], False)

time: 93.8 us -> 88.7 us (0.946)
  waiting for transfers between devices: 30.5 us -> 25.9 us
    all_to_all x1 -> x0, waiting for transfers between devices: 13.1 us -> none  [shards(): lax.all_to_all(outgoing, 'elem', split_axis=3, concat_axis=3, tiled=True)]
    ppermute x0 -> x3, waiting for transfers between devices: none -> 9.59 us  [swapped_with_each(): part = lax.ppermute(part, axis, [(d, d ^ mask) for d in range(ways)])]
    all_to_all x1 -> x0, starting transfers between devices: 4.87 us -> none  [shards(): lax.all_to_all(outgoing, 'elem', split_axis=3, concat_axis=3, tiled=True)]
    ppermute x0 -> x3, starting transfers between devices: none -> 4.45 us  [swapped_with_each(): part = lax.ppermute(part, axis, [(d, d ^ mask) for d in range(ways)])]
  transfers between devices with their start and end apart: 5 -> 7, of which waited for: 5 -> 6; matrix products, arithmetic and copies ran while one was open for 5% -> 6% of each run, Pallas kernels for 0% -> 0%
where the time goes in v1:
time: 88.7 us; the launch traced here: 88.1 us
  waiting for transfers between devices  25.9 us (29%)
  local copies, waits for them, and re-layouts  22.4 us (25%)
  starting transfers between devices  19.9 us (22%)
  matrix products  15.2 us (17%)
  other arithmetic  3.55 us (4%)
  between operations  1.2 us (1%)
    ppermute x3, waiting for transfers between devices, swapped_with_each(): part = lax.ppermute(part, axis, [(d, d ^ mask) for d in range(ways)])  9.59 us
    unnamed x18, local copies, waits for them, and re-layouts  7.63 us
    all_to_all x1, starting transfers between devices, shards(): lax.all_to_all(g_lesser, 'energy', split_axis=2, concat_axis=1, tiled=True)  5.3 us
    ppermute x3, starting transfers between devices, swapped_with_each(): part = lax.ppermute(part, axis, [(d, d ^ mask) for d in range(ways)])  4.45 us
    all_to_all x1, waiting for transfers between devices, shards(): lax.all_to_all(g_greater, 'energy', split_axis=2, concat_axis=1, tiled=True)  4.44 us
    all_to_all x1, waiting for transfers between devices, shards(): lax.all_to_all(result[1], 'energy', split_axis=1, concat_axis=2, tiled=True)  4.29 us
    all_to_all x1, waiting for transfers between devices, shards(): lax.all_to_all(result[0], 'energy', split_axis=1, concat_axis=2, tiled=True)  4.19 us
    all_to_all x1, waiting for transfers between devices, shards(): lax.all_to_all(g_lesser, 'energy', split_axis=2, concat_axis=1, tiled=True)  3.39 us
  transfers between devices with their start and end apart: 7, of which 6 were waited for; matrix products, arithmetic and copies ran while one was open for 6% of the time, Pallas kernels for 0%

profile of v1, /device:TPU:0, one launch (start us, length us, event | category | flops | bytes accessed | tf_op | source)
XLA Modules:
  0.0 88.1 jit_solution(11316423350344994223)
XLA Ops:
  0.6 1.1 %copy.92 = bf16[2,64,512]{1,0,2:T(2,128)(2,1)S(1)} copy(bf16[2,64,512]{2,1,0:T(8,128)(2,1)} %param.4) | data formatting | bytes 262144 | tf_op args[0]
  1.7 0.9 %reshape.175 = bf16[8,2,4096]{2,1,0:T(2,128)(2,1)} reshape(bf16[512,2,64]{2,1,0:T(2,128)(2,1)S(1)} %bitcast.170) | data formatting | bytes 262144
  2.6 5.3 %all-to-all-start = ((bf16[8,2,4096]{2,1,0:T(2,128)(2,1)}), bf16[8,2,4096]{2,1,0:T(2,128)(2,1)S(1)}, u32[]{:S(2)}, u32[]{:S(2)}) async-start(bf16[8,2,4096]{2,1,0:T(2,128)(2,1)} %reshape.175), calls=%async_computation | async-start | bytes 262144 | tf_op jit(solution)/shard_map/all_to_all | solution.py:81
  8.1 0.8 compare_and_fusion.1
  9.1 0.9 %reshape.173 = bf16[8,2,4096]{2,1,0:T(2,128)(2,1)} reshape(bf16[512,2,64]{2,1,0:T(2,128)(2,1)S(1)} %bitcast.171) | data formatting | bytes 262144
  10.1 3.4 %all-to-all-done = bf16[8,2,4096]{2,1,0:T(2,128)(2,1)S(1)} async-done(((bf16[8,2,4096]{2,1,0:T(2,128)(2,1)}), bf16[8,2,4096]{2,1,0:T(2,128)(2,1)S(1)}, u32[]{:S(2)}, u32[]{:S(2)}) %all-to-all-start) | async-done | bytes 131104 | tf_op jit(solution)/shard_map/all_to_all | solution.py:81
  13.5 3.4 %all-to-all-start.1 = ((bf16[8,2,4096]{2,1,0:T(2,128)(2,1)}), bf16[8,2,4096]{2,1,0:T(2,128)(2,1)S(1)}, u32[]{:S(2)}, u32[]{:S(2)}) async-start(bf16[8,2,4096]{2,1,0:T(2,128)(2,1)} %reshape.173), calls=%async_computation.1 | async-start | bytes 262144 | tf_op jit(solution)/shard_map/all_to_all | solution.py:82
  17.9 4.4 %all-to-all-done.1 = bf16[8,2,4096]{2,1,0:T(2,128)(2,1)S(1)} async-done(((bf16[8,2,4096]{2,1,0:T(2,128)(2,1)}), bf16[8,2,4096]{2,1,0:T(2,128)(2,1)S(1)}, u32[]{:S(2)}, u32[]{:S(2)}) %all-to-all-start.1) | async-done | bytes 131104 | tf_op jit(solution)/shard_map/all_to_all | solution.py:82
  23.6 1.7 %gather_fusion = bf16[128,2,2,512]{3,2,1,0:T(2,128)(2,1)S(1)} fusion(bf16[2,2,512,64]{2,1,3,0:T(2,128)(2,1)S(1)} %pad_maximum_fusion.4, s32[1024]{0:T(1024)S(1)} %pad_clamp_fusion.1), kind=kCustom, calls=%fused_computation | custom fusion | bytes 1049088 | tf_op jit(solution)/shard_map/jit(_take)/gather | solution.py:87
  25.3 0.6 broadcast_select_fusion
  26.2 3.7 %collective-permute-start.2 = (bf16[2,2,512,32]{2,1,0,3:T(2,128)(2,1)S(1)}, bf16[2,2,512,32]{2,1,0,3:T(2,128)(2,1)S(1)}, u32[]{:S(2)}, u32[]{:S(2)}) collective-permute-start(bf16[2,2,512,32]{2,1,0,3:T(2,128)(2,1)S(1)} %get-tuple-element.18), channel_id=1, source_target_pairs={{0,3},{1,2},{2,1},{3,0},{4,7},{5,6},{6,5},{7,4},{8,11},{9,10},{10,... | collective-permute-start | bytes 393224 | tf_op jit(solution)/shard_map/ppermute | solution.py:20
  29.9 0.8 collective-permute-start
  31.1 7.0 %collective-permute-done = bf16[2,2,512,32]{2,1,0,3:T(2,128)(2,1)S(1)} collective-permute-done((bf16[2,2,512,32]{2,1,0,3:T(2,128)(2,1)S(1)}, bf16[2,2,512,32]{2,1,0,3:T(2,128)(2,1)S(1)}, u32[]{:S(2)}, u32[]{:S(2)}) %collective-permute-start) | collective-permute-done | bytes 131104 | tf_op jit(solution)/shard_map/ppermute | solution.py:20
  38.2 2.5 %collective-permute-done.1 = bf16[2,2,512,32]{2,1,0,3:T(2,128)(2,1)S(1)} collective-permute-done((bf16[2,2,512,32]{2,1,0,3:T(2,128)(2,1)S(1)}, bf16[2,2,512,32]{2,1,0,3:T(2,128)(2,1)S(1)}, u32[]{:S(2)}, u32[]{:S(2)}) %collective-permute-start.1) | collective-permute-done | bytes 131104 | tf_op jit(solution)/shard_map/ppermute | solution.py:20
  41.0 1.1 %gather_fusion.1 = bf16[64,2,2,512]{3,2,1,0:T(2,128)(2,1)S(1)} fusion(bf16[2,2,512,128]{2,1,3,0:T(2,128)(2,1)S(1)} %copy_dynamic-update-slice_fusion, s32[1024]{0:T(1024)S(1)} %pad_clamp_fusion), kind=kCustom, calls=%fused_computation.1 | custom fusion | bytes 524544 | tf_op jit(solution)/shard_map/jit(_take)/gather | solution.py:89
  42.5 0.7 pad_maximum_fusion.2
  43.2 0.7 fusion.179
  44.5 0.7 copy.106
  45.2 0.6 fusion.34
  45.8 0.6 fusion.38
  46.4 0.6 fusion.3
  47.1 0.9 %multiply_add_fusion = (f32[4,16,32,64]{3,1,2,0:T(8,128)S(1)}, f32[4,16,32,64]{3,1,2,0:T(8,128)S(1)}) fusion(f32[4,16,32,64]{3,1,2,0:T(8,128)S(1)} %fusion.3, f32[16,32]{0,1:T(8,128)S(1)} %get-tuple-element.22, f32[16,32]{0,1:T(8,128)S(1)} %get-tuple-element.23, f32[4,32,64,16]{2,3,1,0:T(8,128)S(1)} %fusion.34, bf16[4,16,32,64]{3,2,1,0:T(8,128)(2,1)S(1)} %bitcast.155), kind=kOutput, calls=%fused_computation.22 | convolution fusion | flops 26087168 | bytes 2363392 | tf_op jit(solution)/shard_map/ka,sabe->skbe/dot_general | solution.py:55
  48.0 1.4 %fusion.12 = f32[4,16,64,32]{2,3,1,0:T(8,128)S(1)} fusion(f32[4,16,32,64]{3,1,2,0:T(8,128)S(1)} %get-tuple-element.4), kind=kOutput, calls=%fused_computation.25 | convolution fusion | flops 50345984 | bytes 1048576 | tf_op jit(solution)/shard_map/qb,skbe->sqke/dot_general | solution.py:65
  49.4 1.4 %fusion.16 = f32[4,16,64,32]{2,3,1,0:T(8,128)S(1)} fusion(f32[4,16,32,64]{3,1,2,0:T(8,128)S(1)} %get-tuple-element.5), kind=kOutput, calls=%fused_computation.29 | convolution fusion | flops 50345984 | bytes 1048576 | tf_op jit(solution)/shard_map/qb,skbe->sqke/dot_general | solution.py:62
  50.8 1.4 %fusion.1 = f32[4,32,16,64]{3,1,2,0:T(8,128)S(1)} fusion(f32[4,16,64,32]{2,3,1,0:T(8,128)S(1)} %fusion.16, f32[4,16,32,64]{3,1,2,0:T(8,128)S(1)} %get-tuple-element.4), kind=kOutput, calls=%fused_computation.5 | convolution fusion | flops 50478080 | bytes 1572864 | tf_op jit(solution)/shard_map/qb,skbe->sqke/dot_general | solution.py:62
  52.2 0.9 %copy-done.1 = f32[4,32,16,64]{3,1,2,0:T(8,128)} copy-done((f32[4,32,16,64]{3,1,2,0:T(8,128)}, f32[4,32,16,64]{3,1,2,0:T(8,128)S(1)}, u32[]{:S(2)}) %copy-start.1) | copy-done | bytes 524312
  53.1 1.4 %fusion = f32[4,32,16,64]{3,1,2,0:T(8,128)S(1)} fusion(f32[4,16,64,32]{2,3,1,0:T(8,128)S(1)} %fusion.12, f32[4,16,32,64]{3,1,2,0:T(8,128)S(1)} %get-tuple-element.5), kind=kOutput, calls=%fused_computation.3 | convolution fusion | flops 50478080 | bytes 1572864 | tf_op jit(solution)/shard_map/qb,skbe->sqke/dot_general | solution.py:65
  54.6 1.0 %copy-done.2 = f32[4,32,16,64]{3,1,2,0:T(8,128)} copy-done((f32[4,32,16,64]{3,1,2,0:T(8,128)}, f32[4,32,16,64]{3,1,2,0:T(8,128)S(1)}, u32[]{:S(2)}) %copy-start.2) | copy-done | bytes 524312
  55.8 0.9 slice-done
  57.2 0.7 slice.80
  58.1 0.9 slice-done.1
  59.5 0.9 slice.89
  60.7 0.9 %fusion.32 = f32[2,32,64,16]{2,3,1,0:T(8,128)S(1)} fusion(f32[2,16,32,64]{3,2,1,0:T(8,128)S(1)} %get-tuple-element.6), kind=kOutput, calls=%fused_computation.60 | convolution fusion | flops 12586496 | bytes 524288 | tf_op jit(solution)/shard_map/ka,sabe->skbe/dot_general | solution.py:52
  61.6 0.9 %fusion.28 = f32[2,32,64,16]{2,3,1,0:T(8,128)S(1)} fusion(f32[2,16,32,64]{3,2,1,0:T(8,128)S(1)} %get-tuple-element.7), kind=kOutput, calls=%fused_computation.56 | convolution fusion | flops 12586496 | bytes 524288 | tf_op jit(solution)/shard_map/ka,sabe->skbe/dot_general | solution.py:55
  62.5 0.9 %fusion.7 = f32[2,16,32,64]{3,1,2,0:T(8,128)S(1)} fusion(f32[2,32,64,16]{2,3,1,0:T(8,128)S(1)} %fusion.32, f32[2,16,32,64]{3,2,1,0:T(8,128)S(1)} %get-tuple-element.7), kind=kOutput, calls=%fused_computation.17 | convolution fusion | flops 12652032 | bytes 786432 | tf_op jit(solution)/shard_map/ka,sabe->skbe/dot_general | solution.py:52
  63.4 1.1 %multiply_subtract_fusion.1 = (f32[2,16,32,64]{3,1,2,0:T(8,128)S(1)}, f32[2,16,32,64]{3,1,2,0:T(8,128)S(1)}) fusion(f32[2,16,32,64]{3,1,2,0:T(8,128)S(1)} %fusion.7, f32[16,32]{0,1:T(8,128)S(1)} %get-tuple-element.23, f32[16,32]{0,1:T(8,128)S(1)} %fusion.89, f32[2,32,64,16]{2,3,1,0:T(8,128)S(1)} %fusion.28, f32[2,16,32,64]{3,2,1,0:T(8,128)S(1)} %get-tuple-element.6), kind=kOutput, calls=%fused_computation.47 | convolution fusion | flops 13045248 | bytes 1314816 | tf_op jit(solution)/shard_map/ka,sabe->skbe/dot_general | solution.py:55
  64.5 0.8 fusion.22
  65.2 0.8 fusion.26
  66.0 0.8 fusion.10
  66.8 0.8 fusion.11
  68.2 0.9 %reshape.179 = bf16[8,2,4096]{2,1,0:T(2,128)(2,1)} reshape(bf16[512,2,64]{2,1,0:T(2,128)(2,1)S(1)} %bitcast.176) | data formatting | bytes 262144
  69.1 3.4 %all-to-all-start.3 = ((bf16[8,2,4096]{2,1,0:T(2,128)(2,1)}), bf16[8,2,4096]{2,1,0:T(2,128)(2,1)S(1)}, u32[]{:S(2)}, u32[]{:S(2)}) async-start(bf16[8,2,4096]{2,1,0:T(2,128)(2,1)} %reshape.179), calls=%async_computation.3 | async-start | bytes 262144 | tf_op jit(solution)/shard_map/all_to_all | solution.py:104
  72.8 0.9 %reshape.177 = bf16[8,2,4096]{2,1,0:T(2,128)(2,1)} reshape(bf16[512,2,64]{2,1,0:T(2,128)(2,1)S(1)} %bitcast.177) | data formatting | bytes 262144
  73.7 4.3 %all-to-all-done.3 = bf16[8,2,4096]{2,1,0:T(2,128)(2,1)S(1)} async-done(((bf16[8,2,4096]{2,1,0:T(2,128)(2,1)}), bf16[8,2,4096]{2,1,0:T(2,128)(2,1)S(1)}, u32[]{:S(2)}, u32[]{:S(2)}) %all-to-all-start.3) | async-done | bytes 131104 | tf_op jit(solution)/shard_map/all_to_all | solution.py:104
  78.0 3.4 %all-to-all-start.2 = ((bf16[8,2,4096]{2,1,0:T(2,128)(2,1)}), bf16[8,2,4096]{2,1,0:T(2,128)(2,1)S(1)}, u32[]{:S(2)}, u32[]{:S(2)}) async-start(bf16[8,2,4096]{2,1,0:T(2,128)(2,1)} %reshape.177), calls=%async_computation.2 | async-start | bytes 262144 | tf_op jit(solution)/shard_map/all_to_all | solution.py:103
  81.7 0.9 all_to_all.61
  82.6 4.2 %all-to-all-done.2 = bf16[8,2,4096]{2,1,0:T(2,128)(2,1)S(1)} async-done(((bf16[8,2,4096]{2,1,0:T(2,128)(2,1)}), bf16[8,2,4096]{2,1,0:T(2,128)(2,1)S(1)}, u32[]{:S(2)}, u32[]{:S(2)}) %all-to-all-start.2) | async-done | bytes 131104 | tf_op jit(solution)/shard_map/all_to_all | solution.py:103
  87.2 0.9 all_to_all.57
  (61 shorter events, 8.0 us)
Async XLA Ops:
  0.6 7.3 %copy-start = (s32[1,8,4,32]{3,2,1,0:T(4,128)S(1)}, s32[1,8,4,32]{3,2,1,0:T(4,128)}, u32[]{:S(2)}) copy-start(s32[1,8,4,32]{3,2,1,0:T(4,128)} %param.6) | copy-start | bytes 12292
  2.6 6.3 %copy-start.3 = (bf16[2,64,512]{2,1,0:T(8,128)(2,1)S(1)}, bf16[2,64,512]{2,1,0:T(8,128)(2,1)}, u32[]{:S(2)}) copy-start(bf16[2,64,512]{2,1,0:T(8,128)(2,1)} %param.5) | copy-start | bytes 393220
  2.6 10.8 %all-to-all-start = ((bf16[8,2,4096]{2,1,0:T(2,128)(2,1)}), bf16[8,2,4096]{2,1,0:T(2,128)(2,1)S(1)}, u32[]{:S(2)}, u32[]{:S(2)}) async-start(bf16[8,2,4096]{2,1,0:T(2,128)(2,1)} %reshape.175), calls=%async_computation | async-start | bytes 262144 | tf_op jit(solution)/shard_map/all_to_all | solution.py:81
  13.5 8.8 %all-to-all-start.1 = ((bf16[8,2,4096]{2,1,0:T(2,128)(2,1)}), bf16[8,2,4096]{2,1,0:T(2,128)(2,1)S(1)}, u32[]{:S(2)}, u32[]{:S(2)}) async-start(bf16[8,2,4096]{2,1,0:T(2,128)(2,1)} %reshape.173), calls=%async_computation.1 | async-start | bytes 262144 | tf_op jit(solution)/shard_map/all_to_all | solution.py:82
  26.2 14.7 %collective-permute-start.2 = (bf16[2,2,512,32]{2,1,0,3:T(2,128)(2,1)S(1)}, bf16[2,2,512,32]{2,1,0,3:T(2,128)(2,1)S(1)}, u32[]{:S(2)}, u32[]{:S(2)}) collective-permute-start(bf16[2,2,512,32]{2,1,0,3:T(2,128)(2,1)S(1)} %get-tuple-element.18), channel_id=1, source_target_pairs={{0,3},{1,2},{2,1},{3,0},{4,7},{5,6},{6,5},{7,4},{8,11},{9,10},{10,... | collective-permute-start | bytes 393224 | tf_op jit(solution)/shard_map/ppermute | solution.py:20
  29.9 10.9 %collective-permute-start.1 = (bf16[2,2,512,32]{2,1,0,3:T(2,128)(2,1)S(1)}, bf16[2,2,512,32]{2,1,0,3:T(2,128)(2,1)S(1)}, u32[]{:S(2)}, u32[]{:S(2)}) collective-permute-start(bf16[2,2,512,32]{2,1,0,3:T(2,128)(2,1)S(1)} %get-tuple-element.19), channel_id=1, source_target_pairs={{0,2},{1,3},{2,0},{3,1},{4,6},{5,7},{6,4},{7,5},{8,10},{9,11},{10,... | collective-permute-start | bytes 393224 | tf_op jit(solution)/shard_map/ppermute | solution.py:20
  29.9 8.2 %collective-permute-start = (bf16[2,2,512,32]{2,1,0,3:T(2,128)(2,1)S(1)}, bf16[2,2,512,32]{2,1,0,3:T(2,128)(2,1)S(1)}, u32[]{:S(2)}, u32[]{:S(2)}) collective-permute-start(bf16[2,2,512,32]{2,1,0,3:T(2,128)(2,1)S(1)} %get-tuple-element.20), channel_id=1, source_target_pairs={{0,1},{1,0},{2,3},{3,2},{4,5},{5,4},{6,7},{7,6},{8,9},{9,8},{10,11... | collective-permute-start | bytes 393224 | tf_op jit(solution)/shard_map/ppermute | solution.py:20
  52.2 1.0 %copy-start.1 = (f32[4,32,16,64]{3,1,2,0:T(8,128)}, f32[4,32,16,64]{3,1,2,0:T(8,128)S(1)}, u32[]{:S(2)}) copy-start(f32[4,32,16,64]{3,1,2,0:T(8,128)S(1)} %fusion.1) | copy-start | bytes 1572868
  54.5 1.0 %copy-start.2 = (f32[4,32,16,64]{3,1,2,0:T(8,128)}, f32[4,32,16,64]{3,1,2,0:T(8,128)S(1)}, u32[]{:S(2)}) copy-start(f32[4,32,16,64]{3,1,2,0:T(8,128)S(1)} %fusion) | copy-start | bytes 1572868
  55.6 1.0 %slice-start = ((f32[4,32,16,64]{3,1,2,0:T(8,128)}), f32[2,32,16,64]{3,1,2,0:T(8,128)S(1)}, s32[]{:S(2)}) async-start(f32[4,32,16,64]{3,1,2,0:T(8,128)} %copy-done.1), calls=%async_computation.4 | async-start | bytes 1048576 | tf_op jit(solution)/shard_map/slice | solution.py:92
  57.9 1.0 %slice-start.1 = ((f32[4,32,16,64]{3,1,2,0:T(8,128)}), f32[2,32,16,64]{3,1,2,0:T(8,128)S(1)}, s32[]{:S(2)}) async-start(f32[4,32,16,64]{3,1,2,0:T(8,128)} %copy-done.2), calls=%async_computation.5 | async-start | bytes 1048576 | tf_op jit(solution)/shard_map/slice | solution.py:93
  69.1 8.8 %all-to-all-start.3 = ((bf16[8,2,4096]{2,1,0:T(2,128)(2,1)}), bf16[8,2,4096]{2,1,0:T(2,128)(2,1)S(1)}, u32[]{:S(2)}, u32[]{:S(2)}) async-start(bf16[8,2,4096]{2,1,0:T(2,128)(2,1)} %reshape.179), calls=%async_computation.3 | async-start | bytes 262144 | tf_op jit(solution)/shard_map/all_to_all | solution.py:104
  78.0 8.8 %all-to-all-start.2 = ((bf16[8,2,4096]{2,1,0:T(2,128)(2,1)}), bf16[8,2,4096]{2,1,0:T(2,128)(2,1)S(1)}, u32[]{:S(2)}, u32[]{:S(2)}) async-start(bf16[8,2,4096]{2,1,0:T(2,128)(2,1)} %reshape.177), calls=%async_computation.2 | async-start | bytes 262144 | tf_op jit(solution)/shard_map/all_to_all | solution.py:103
